TPU v7x, 512 devices: a whole 4x4x16 slice. The times are simulated.
512 devices in a mesh: node: 64 (over y, z), local: 8 (over x, core).
Axes of the slice: x: 4, y: 4, z: 16, core: 2. Of those that a mesh axis runs over, the one named last changes fastest.
Arguments:
- grad_out: bfloat16 [65536, 3584], P(('node', 'local')), may hold values from -6 to 6
- expert_ids: int32 [65536, 8], P(('node', 'local')), may hold values from 0 to 255, as said below
- gate_weights: float32 [65536, 8], P(('node', 'local')), may hold values from 0.05 to 0.35
- saved_hidden: bfloat16 [64, 1024, 1024], P('node', None, 'local'), may hold values from -0.59765625 to 0.59765625
- down_weight: bfloat16 [64, 1024, 3584], P('node', 'local'), may hold values from -0.1875 to 0.1875
- second_moment: bfloat16 [64, 1024, 3584], P('node', 'local'), may hold values from 0.0019989014 to 0.25
Outputs:
- gate_weight_gradient: float32 [65536, 8], P(('node', 'local'))
- hidden_grad: bfloat16 [64, 1024, 1024], P('node', None, 'local')
- new_weight: bfloat16 [64, 1024, 3584], P('node', 'local')
- new_second: bfloat16 [64, 1024, 3584], P('node', 'local')
Inputs may be any that keep to these rules, and one draw needn't show every extreme that they name: `expert_ids`: each row names 8 different experts on at most 4 nodes (node = id // 4), two on each; at most one per row is in flight (id % 4 == 0). Among the rows of one device at most 2 name the in-flight expert of any one node, and in every draw some node receives exactly 2 from every device.
All inputs are finite; a program needn't handle non-finite values.
Results may differ from a plain program's by a relative error of at most 0.0051.
Values may be sent and summed in bfloat16 or wider, within the bound.
No kernel may reach another device: no remote copies, remote signals or barrier semaphores. Data moves between devices by JAX's collectives and lax.ppermute only.
A program may use at most 128 MiB of HBM per device.

v0:
```python
import jax
import jax.numpy as jnp
from jax import lax
from jax.sharding import PartitionSpec as P

EXPERTS_PER_HOST = 4
CAP = 2
beta_second = 0.95
learn_rate = 0.002
decay_rate = 0.1
epsilon = 1e-08
correct_second = 0.994079470779666


def route(picked_experts, gate_values, node_count):
    transit_rows = picked_experts % EXPERTS_PER_HOST == 0
    row_present = jnp.any(transit_rows, 1)
    destination_node = jnp.sum(jnp.where(transit_rows, picked_experts // EXPERTS_PER_HOST, 0), 1)
    tokens = picked_experts.shape[0]
    same = (
        (destination_node[:, None] == destination_node[None, :])
        & row_present[None, :]
        & (jnp.arange(tokens)[None, :] < jnp.arange(tokens)[:, None])
    )
    within_rank = jnp.sum(same.astype(jnp.int32), 1)
    slot_index = destination_node * CAP + within_rank
    expert_location = (
        jnp.arange(node_count * CAP, dtype=jnp.int32)[:, None] == slot_index[None, :]
    ) & row_present[None, :]
    matched_gate = jnp.sum(jnp.where(transit_rows, gate_values, 0.0), 1).astype(jnp.bfloat16)
    return (expert_location, transit_rows, row_present, matched_gate.astype(jnp.float32))


def on_device(grad_out, expert_ids, gate_weights, saved_hidden, down_weight, second_moment):
    node_count = lax.axis_size("node")
    members = lax.axis_size("local")
    feature_count = grad_out.shape[1]
    expert_location, transit_rows, row_present, gate = route(expert_ids, gate_weights, node_count)
    slot_gate = jnp.sum(jnp.where(expert_location, gate[None, :], 0.0), 1)
    picked = jnp.dot(
        expert_location.astype(jnp.bfloat16), grad_out, preferred_element_type=jnp.float32
    )
    scaled_out = (slot_gate[:, None] * picked).astype(jnp.bfloat16)
    arrived = lax.all_to_all(
        scaled_out.reshape(node_count, CAP, feature_count),
        "node",
        split_axis=0,
        concat_axis=0,
        tiled=True,
    )
    scaled = lax.all_gather(
        arrived.reshape(node_count * CAP, feature_count), "local", axis=0, tiled=True
    )
    weight_now = down_weight[0]
    hidden_now = saved_hidden[0]
    hidden_f = lax.dot_general(
        scaled, weight_now, (((1,), (1,)), ((), ())), preferred_element_type=jnp.float32
    )
    slot_score = jnp.sum(hidden_f * hidden_now.astype(jnp.float32), 1)
    grad = lax.dot_general(
        hidden_now, scaled, (((0,), (0,)), ((), ())), preferred_element_type=jnp.float32
    )
    second_new = (
        beta_second * second_moment[0].astype(jnp.float32) + (1.0 - beta_second) * grad * grad
    )
    weight_f = weight_now.astype(jnp.float32)
    update = grad / (jnp.sqrt(second_new / correct_second) + epsilon) + decay_rate * weight_f
    weight_new = weight_f - learn_rate * update
    score_terms = slot_score.reshape(members, node_count * CAP)
    summed = lax.psum(score_terms, "local")
    own_terms = lax.dynamic_slice_in_dim(summed, lax.axis_index("local"), 1, 0)
    returned = lax.all_to_all(
        own_terms.reshape(node_count, CAP), "node", split_axis=0, concat_axis=0, tiled=True
    )
    returned_flat = returned.reshape(node_count * CAP)
    token_score = jnp.sum(jnp.where(expert_location, returned_flat[:, None], 0.0), 0)
    token_gradient = jnp.where(row_present, token_score / jnp.where(row_present, gate, 1.0), 0.0)
    gate_weight_gradient = jnp.where(transit_rows, token_gradient[:, None], 0.0)
    return (
        gate_weight_gradient,
        hidden_f.astype(jnp.bfloat16)[None],
        weight_new.astype(jnp.bfloat16)[None],
        second_new.astype(jnp.bfloat16)[None],
    )


def solution(mesh):
    return jax.shard_map(
        on_device,
        mesh=mesh,
        in_specs=(
            P(("node", "local"), None),
            P(("node", "local"), None),
            P(("node", "local"), None),
            P("node", None, "local"),
            P("node", "local", None),
            P("node", "local", None),
        ),
        out_specs=(
            P(("node", "local"), None),
            P("node", None, "local"),
            P("node", "local", None),
            P("node", "local", None),
        ),
        check_vma=False,
    )
```

profile of v0, /device:TPU:8, one launch (start us, length us, event | category | flops | bytes accessed | tf_op | source)
XLA Modules:
  0.0 181.2 jit_solution(6624401985966689629)
XLA Ops:
  7.2 0.0 copy-start
  7.2 0.0 all-gather.2.cloned.1.call-start
  7.2 0.8 fusion.18
  8.0 0.7 select_reduce_fusion.2
  8.7 0.2 convert_reduce_fusion
  8.9 0.1 select_reduce_fusion.1
  9.0 0.3 copy-done.5
  9.3 0.0 copy-done
  9.3 0.4 fusion
  9.7 0.3 reshape.51
  10.1 66.9 %all_to_all.14 = bf16[64,2,3584]{2,1,0:T(2,128)(2,1)S(1)} all-to-all(bf16[64,2,3584]{2,1,0:T(2,128)(2,1)S(1)} %reshape.51), channel_id=1, replica_groups=mesh['node'=64,'local'=8] {'node'}, dimensions={0} | all-to-all | bytes 1835008 | tf_op jit(solution)/shard_map/all_to_all | solution.py:44
  77.0 1.3 reshape.52
  78.3 0.0 all-gather.2.cloned.1.call-update
  78.3 0.1 copy.30
  78.5 1.3 copy.32
  79.7 1.3 copy.29
  81.0 42.7 %all-gather.2.cloned.1.call-done = bf16[1024,3584]{1,0:T(8,128)(2,1)} async-done(((bf16[128,3584]{1,0:T(8,128)(2,1)}), bf16[1024,3584]{1,0:T(8,128)(2,1)}) %all-gather.2.cloned.1.call-update) | async-done | bytes 7340048 | tf_op jit(solution)/shard_map/all_gather | solution.py:51
  123.7 5.5 %convert_bitcast_fusion = (bf16[1,1024,128]{1,2,0:T(8,128)(2,1)S(1)}, f32[1024]{0:T(1024)S(1)}) fusion(bf16[1,1024,128]{1,2,0:T(8,128)(2,1)S(1)} %copy.30, bf16[1024,3584]{1,0:T(8,128)(2,1)} %all-gather.2.cloned.1.call-done, bf16[1,128,3584]{2,1,0:T(8,128)(2,1)S(1)} %copy-done.2), kind=kOutput, calls=%fused_computation.17 | convolution fusion | flops 940047360 | bytes 8785920 | tf_op jit(solution)/shard_map/dot_general | solution.py:56
  129.2 13.2 %psum.7 = f32[8,128]{1,0:T(8,128)S(1)} all-reduce(f32[8,128]{1,0:T(8,128)S(1)} %bitcast.41), channel_id=1, replica_groups=mesh['node'=64,'local'=8] {'local'}, use_global_device_ids=true, to_apply=%region_6.7 | all-reduce | flops 1024 | bytes 8192 | tf_op jit(solution)/shard_map/psum | solution.py:70
  142.4 0.7 all_to_all.10
  143.2 15.8 %all-to-all-start.1 = ((f32[64,1,2]{2,1,0:T(1,128)}), f32[64,1,2]{2,1,0:T(1,128)S(1)}, u32[]{:S(2)}, u32[]{:S(2)}) async-start(f32[64,1,2]{2,1,0:T(1,128)} %bitcast.3), calls=%async_computation.1 | async-start | bytes 65536 | tf_op jit(solution)/shard_map/all_to_all | solution.py:72
  158.9 7.2 %fusion.6 = (bf16[1,128,3584]{1,2,0:T(8,128)(2,1)}, bf16[1,128,3584]{1,2,0:T(8,128)(2,1)S(1)}) fusion(bf16[1,128,3584]{1,2,0:T(8,128)(2,1)S(1)} %copy-done.3, bf16[1,128,3584]{1,2,0:T(8,128)(2,1)} %copy.29, bf16[1024,3584]{1,0:T(8,128)(2,1)} %all-gather.2.cloned.1.call-done, bf16[1,1024,128]{2,1,0:T(8,128)(2,1)S(1)} %copy-done.4), kind=kOutput, calls=%fused_computation.11 | convolution fusion | flops 946405376 | bytes 11272192 | tf_op jit(solution)/shard_map/dot_general | solution.py:60
  166.1 0.8 copy.33
  167.0 2.2 %copy.35 = bf16[1,128,3584]{2,1,0:T(8,128)(2,1)} copy(bf16[1,128,3584]{1,2,0:T(8,128)(2,1)} %get-tuple-element.22) | data formatting | bytes 1835008
  169.2 1.3 copy.34
  170.5 1.8 %all-to-all-done.1 = f32[64,1,2]{2,1,0:T(1,128)S(1)} async-done(((f32[64,1,2]{2,1,0:T(1,128)}), f32[64,1,2]{2,1,0:T(1,128)S(1)}, u32[]{:S(2)}, u32[]{:S(2)}) %all-to-all-start.1) | async-done | bytes 544 | tf_op jit(solution)/shard_map/all_to_all | solution.py:72
  172.3 0.5 broadcast.39
  172.8 0.7 reduce.7
  173.5 0.1 broadcast_in_dim.70
  173.7 0.1 select_reduce_fusion
  173.8 0.0 copy-done.6
  173.8 0.6 broadcast_select_fusion
  (15 shorter events, 0.1 us)
Async XLA Ops:
  7.2 2.1 %copy-start = (bf16[128,3584]{1,0:T(8,128)(2,1)S(1)}, bf16[128,3584]{1,0:T(8,128)(2,1)}, u32[]{:S(2)}) copy-start(bf16[128,3584]{1,0:T(8,128)(2,1)} %param.6) | copy-start | bytes 2752516
  7.2 116.5 %all-gather.2.cloned.1.call-start = ((), (), s32[]{:S(2)}) async-start(), calls=%async_computation.2 | async-start | bytes 8257536 | tf_op jit(solution)/shard_map/all_gather | solution.py:51
  8.7 0.6 copy-start.5
  77.0 1.3 copy-start.4
  77.0 1.5 copy-start.1
  78.3 1.5 copy-start.2
  81.0 77.9 %copy-start.3 = (bf16[1,128,3584]{1,2,0:T(8,128)(2,1)S(1)}, bf16[1,128,3584]{1,2,0:T(8,128)(2,1)}, u32[]{:S(2)}) copy-start(bf16[1,128,3584]{1,2,0:T(8,128)(2,1)} %copy.32) | copy-start | bytes 2752516
  143.2 29.1 %all-to-all-start.1 = ((f32[64,1,2]{2,1,0:T(1,128)}), f32[64,1,2]{2,1,0:T(1,128)S(1)}, u32[]{:S(2)}, u32[]{:S(2)}) async-start(f32[64,1,2]{2,1,0:T(1,128)} %bitcast.3), calls=%async_computation.1 | async-start | bytes 65536 | tf_op jit(solution)/shard_map/all_to_all | solution.py:72
  167.0 6.8 %copy-start.6 = (bf16[128]{0:T(256)(128)(2,1)S(1)}, bf16[128]{0:T(256)(128)(2,1)}, u32[]{:S(2)}) copy-start(bf16[128]{0:T(256)(128)(2,1)} %copy-done.5) | copy-start | bytes 772
Sparse Core Ops, SparseCore 0:
  78.4 45.2 all-gather.1
where the time goes:
time: 182 us; the launch traced here: 181 us
  blocking collectives  80.1 us (44%)
  waiting for transfers between devices  44.5 us (24%)
  starting transfers between devices  15.8 us (9%)
  between operations  14.2 us (8%)
  matrix products  13.1 us (7%)
  local copies, waits for them, and re-layouts  10.3 us (6%)
  other arithmetic  3.23 us (2%)
    all_to_all x1, blocking collectives, on_device(): lax.all_to_all(scaled_out.reshape(node_count, CAP, feature_count), 'node'...  66.9 us
    all_gather x1, waiting for transfers between devices, on_device(): lax.all_gather(arrived.reshape(node_count * CAP, feature_count), 'local',...  42.7 us
    all_to_all x1, starting transfers between devices, on_device(): lax.all_to_all(own_terms.reshape(node_count, CAP), 'node', split_axis=0,...  15.8 us
    psum x1, blocking collectives, on_device(): summed = lax.psum(score_terms, 'local')  13.2 us
    unnamed x20, local copies, waits for them, and re-layouts  7.28 us
    dot_general x1, matrix products, on_device(): lax.dot_general(hidden_now, scaled, (((0,), (0,)), ((), ())), preferred_e...  7.21 us
    dot_general x1, matrix products, on_device(): lax.dot_general(scaled, weight_now, (((1,), (1,)), ((), ())), preferred_e...  5.51 us
  transfers between devices with their start and end apart: 2, of which 2 were waited for; matrix products, arithmetic and copies ran while one was open for 8% of the time, Pallas kernels for 0%

commit v1 on v0

--- a/solution.py
+++ b/solution.py
@@ -48,8 +48,14 @@
         concat_axis=0,
         tiled=True,
     )
-    scaled = lax.all_gather(
-        arrived.reshape(node_count * CAP, feature_count), "local", axis=0, tiled=True
+    scaled = jnp.concatenate(
+        lax.all_to_all(
+            jnp.stack([arrived.reshape(node_count * CAP, feature_count)] * lax.axis_size("local")),
+            "local",
+            0,
+            0,
+        ),
+        axis=0,
     )
     weight_now = down_weight[0]
     hidden_now = saved_hidden[0]

time: 182 us -> 205 us (1.13)
  the two profiles are of different devices: /device:TPU:8 before, /device:TPU:1 now
where the time goes in v1:
time: 205 us; the launch traced here: 204 us
  waiting for transfers between devices  81.6 us (40%)
  blocking collectives  77.2 us (38%)
  starting transfers between devices  15.1 us (7%)
  local copies, waits for them, and re-layouts  13.3 us (6%)
  matrix products  13.2 us (6%)
  other arithmetic  3.24 us (2%)
    all_to_all x1, waiting for transfers between devices, on_device(): lax.all_to_all(jnp.stack([arrived.reshape(node_count * CAP, feature_count...  79.9 us
    all_to_all x1, blocking collectives, on_device(): lax.all_to_all(scaled_out.reshape(node_count, CAP, feature_count), 'node'...  64.6 us
    psum x1, blocking collectives, on_device(): summed = lax.psum(score_terms, 'local')  12.6 us
    all_to_all x1, starting transfers between devices, on_device(): lax.all_to_all(jnp.stack([arrived.reshape(node_count * CAP, feature_count...  8.81 us
    unnamed x20, local copies, waits for them, and re-layouts  7.59 us
    dot_general x1, matrix products, on_device(): lax.dot_general(hidden_now, scaled, (((0,), (0,)), ((), ())), preferred_e...  7.23 us
    all_to_all x1, starting transfers between devices, on_device(): lax.all_to_all(own_terms.reshape(node_count, CAP), 'node', split_axis=0,...  6.28 us
    dot_general x1, matrix products, on_device(): lax.dot_general(scaled, weight_now, (((1,), (1,)), ((), ())), preferred_e...  5.6 us
  transfers between devices with their start and end apart: 2, of which 2 were waited for; matrix products, arithmetic and copies ran while one was open for 7% of the time, Pallas kernels for 0%

profile of v1, /device:TPU:1, one launch (start us, length us, event | category | flops | bytes accessed | tf_op | source)
XLA Modules:
  0.0 204.5 jit_solution(8396040006974670567)
XLA Ops:
  0.6 0.0 copy-start
  0.6 0.8 fusion.18
  1.5 0.2 convert_reduce_fusion
  1.6 0.7 select_reduce_fusion.2
  2.4 0.6 copy-done.5
  2.9 0.1 select_reduce_fusion.1
  3.0 0.0 copy-done
  3.1 0.4 fusion
  3.5 0.3 reshape.53
  3.8 64.6 %all_to_all.19 = bf16[64,2,3584]{2,1,0:T(2,128)(2,1)S(1)} all-to-all(bf16[64,2,3584]{2,1,0:T(2,128)(2,1)S(1)} %reshape.53), channel_id=1, replica_groups=mesh['node'=64,'local'=8] {'node'}, dimensions={0} | all-to-all | bytes 1835008 | tf_op jit(solution)/shard_map/all_to_all | solution.py:44
  68.4 0.3 stack_reshape.2
  68.7 3.6 %stack.3 = bf16[8,128,3584]{2,1,0:T(8,128)(2,1)} broadcast(bf16[128,3584]{1,0:T(8,128)(2,1)S(1)} %stack_reshape.2), dimensions={1,2} | broadcast | bytes 8257536 | tf_op jit(solution)/shard_map/stack | solution.py:53
  72.4 8.8 %all-to-all-start.1 = ((bf16[8,128,3584]{2,1,0:T(8,128)(2,1)}), bf16[8,128,3584]{2,1,0:T(8,128)(2,1)}, u32[]{:S(2)}, u32[]{:S(2)}) async-start(bf16[8,128,3584]{2,1,0:T(8,128)(2,1)} %stack.3), calls=%async_computation.1 | async-start | bytes 14680064 | tf_op jit(solution)/shard_map/all_to_all | solution.py:52
  81.2 0.1 copy.30
  81.3 1.3 copy.29
  82.6 0.0 copy-done.1
  82.6 1.3 copy.32
  83.9 79.9 %all-to-all-done.1 = bf16[8,128,3584]{2,1,0:T(8,128)(2,1)} async-done(((bf16[8,128,3584]{2,1,0:T(8,128)(2,1)}), bf16[8,128,3584]{2,1,0:T(8,128)(2,1)}, u32[]{:S(2)}, u32[]{:S(2)}) %all-to-all-start.1) | async-done | bytes 7340064 | tf_op jit(solution)/shard_map/all_to_all | solution.py:52
  163.8 5.6 %convert_bitcast_fusion = (bf16[1,1024,128]{1,2,0:T(8,128)(2,1)S(1)}, f32[1024]{0:T(1024)S(1)}) fusion(bf16[1,1024,128]{1,2,0:T(8,128)(2,1)S(1)} %copy.30, bf16[1024,3584]{1,0:T(8,128)(2,1)} %bitcast, bf16[1,128,3584]{2,1,0:T(8,128)(2,1)S(1)} %copy-done.2), kind=kOutput, calls=%fused_computation.17 | convolution fusion | flops 940047360 | bytes 8785920 | tf_op jit(solution)/shard_map/dot_general | solution.py:62
  169.4 12.6 %psum.7 = f32[8,128]{1,0:T(8,128)S(1)} all-reduce(f32[8,128]{1,0:T(8,128)S(1)} %bitcast.42), channel_id=1, replica_groups=mesh['node'=64,'local'=8] {'local'}, use_global_device_ids=true, to_apply=%region_6.7 | all-reduce | flops 1024 | bytes 8192 | tf_op jit(solution)/shard_map/psum | solution.py:76
  182.1 0.7 all_to_all.14
  182.8 6.3 %all-to-all-start.2 = ((f32[64,1,2]{2,1,0:T(1,128)}), f32[64,1,2]{2,1,0:T(1,128)S(1)}, u32[]{:S(2)}, u32[]{:S(2)}) async-start(f32[64,1,2]{2,1,0:T(1,128)} %bitcast.4), calls=%async_computation.2 | async-start | bytes 65536 | tf_op jit(solution)/shard_map/all_to_all | solution.py:78
  189.1 7.2 %fusion.6 = (bf16[1,128,3584]{1,2,0:T(8,128)(2,1)S(1)}, bf16[1,128,3584]{1,2,0:T(8,128)(2,1)}) fusion(bf16[1,128,3584]{1,2,0:T(8,128)(2,1)} %copy.32, bf16[1,128,3584]{1,2,0:T(8,128)(2,1)S(1)} %copy-done.3, bf16[1024,3584]{1,0:T(8,128)(2,1)} %bitcast, bf16[1,1024,128]{2,1,0:T(8,128)(2,1)S(1)} %copy-done.4), kind=kOutput, calls=%fused_computation.11 | convolution fusion | flops 946405376 | bytes 11272192 | tf_op jit(solution)/shard_map/dot_general | solution.py:66
  196.3 2.2 %copy.34 = bf16[1,128,3584]{2,1,0:T(8,128)(2,1)} copy(bf16[1,128,3584]{1,2,0:T(8,128)(2,1)} %get-tuple-element.23) | data formatting | bytes 1835008
  198.6 1.3 copy.35
  199.8 0.8 copy.33
  200.7 1.7 all-to-all-done.2
  202.4 0.5 broadcast.40
  202.9 0.7 reduce.7
  203.6 0.1 broadcast_in_dim.70
  203.7 0.1 select_reduce_fusion
  203.9 0.6 broadcast_select_fusion
  (15 shorter events, 0.1 us)
Async XLA Ops:
  0.6 2.4 %copy-start = (bf16[128,3584]{1,0:T(8,128)(2,1)S(1)}, bf16[128,3584]{1,0:T(8,128)(2,1)}, u32[]{:S(2)}) copy-start(bf16[128,3584]{1,0:T(8,128)(2,1)} %param.6) | copy-start | bytes 2752516
  2.4 0.6 copy-start.5
  72.4 8.8 %copy-start.4 = (bf16[1,1024,128]{2,1,0:T(8,128)(2,1)S(1)}, bf16[1,1024,128]{2,1,0:T(8,128)(2,1)}, u32[]{:S(2)}) copy-start(bf16[1,1024,128]{2,1,0:T(8,128)(2,1)} %param.9) | copy-start | bytes 786436
  72.4 9.0 %copy-start.2 = (bf16[1,128,3584]{2,1,0:T(8,128)(2,1)S(1)}, bf16[1,128,3584]{2,1,0:T(8,128)(2,1)}, u32[]{:S(2)}) copy-start(bf16[1,128,3584]{2,1,0:T(8,128)(2,1)} %param.10) | copy-start | bytes 2752516
  72.4 91.4 %all-to-all-start.1 = ((bf16[8,128,3584]{2,1,0:T(8,128)(2,1)}), bf16[8,128,3584]{2,1,0:T(8,128)(2,1)}, u32[]{:S(2)}, u32[]{:S(2)}) async-start(bf16[8,128,3584]{2,1,0:T(8,128)(2,1)} %stack.3), calls=%async_computation.1 | async-start | bytes 14680064 | tf_op jit(solution)/shard_map/all_to_all | solution.py:52
  81.2 1.4 copy-start.1
  163.8 25.3 %copy-start.3 = (bf16[1,128,3584]{1,2,0:T(8,128)(2,1)S(1)}, bf16[1,128,3584]{1,2,0:T(8,128)(2,1)}, u32[]{:S(2)}) copy-start(bf16[1,128,3584]{1,2,0:T(8,128)(2,1)} %copy.29) | copy-start | bytes 2752516
  182.8 19.5 %all-to-all-start.2 = ((f32[64,1,2]{2,1,0:T(1,128)}), f32[64,1,2]{2,1,0:T(1,128)S(1)}, u32[]{:S(2)}, u32[]{:S(2)}) async-start(f32[64,1,2]{2,1,0:T(1,128)} %bitcast.4), calls=%async_computation.2 | async-start | bytes 65536 | tf_op jit(solution)/shard_map/all_to_all | solution.py:78
  196.3 7.5 %copy-start.6 = (bf16[128]{0:T(256)(128)(2,1)S(1)}, bf16[128]{0:T(256)(128)(2,1)}, u32[]{:S(2)}) copy-start(bf16[128]{0:T(256)(128)(2,1)} %copy-done.5) | copy-start | bytes 772
